TPU v7x, 256 devices: a whole 4x4x8 slice. The times are simulated.
256 devices in a mesh: pix: 32 (over z_hi, y, x), tm: 8 (over z_lo, core).
Axes of the slice: x: 4, y: 4, z: 8 (z_hi: 2, z_lo: 4; z = z_hi * 4 + z_lo), core: 2. Of those that a mesh axis runs over, the one named last changes fastest.
Arguments:
- fields: float32 [256, 8, 2, 1024], P('pix', None, None, 'tm'), may hold values from -6 to 6
- profiles: bfloat16 [65536, 256], P('pix'), may hold values from -0.75 to 0.75
- phase: float32 [256, 1024], P(('pix', 'tm')), may hold values from -3.140625 to 3.140625
Outputs:
- advanced: float32 [256, 8, 2, 1024], P('pix', None, None, 'tm')
All inputs are finite; a program needn't handle non-finite values.
Results may differ from a plain program's by a relative error of at most 0.003.
Values may be sent and summed in bfloat16 or wider, within the bound.
A program may use at most 64 MiB of HBM per device.

v0:
```python
import math
import jax
import jax.numpy as jnp
from jax import lax
from jax.sharding import PartitionSpec as P


def joined_along(blocks, dim):
    blocks = jnp.moveaxis(blocks, 0, dim)
    dims = blocks.shape
    return blocks.reshape(*dims[:dim], dims[dim] * dims[dim + 1], *dims[dim + 2 :])


def copy_for_each(value, axis):
    devices = lax.axis_size(axis)
    return lax.all_to_all(
        jnp.broadcast_to(value[None], (devices, *value.shape)), axis, 0, 0, tiled=True
    )


def gathered_copies(value, axis, dim):
    return joined_along(copy_for_each(value, axis), dim)


def in_blocks(value, dim, devices):
    dims = value.shape
    blocks = value.reshape(*dims[:dim], devices, dims[dim] // devices, *dims[dim + 1 :])
    return jnp.moveaxis(blocks, dim, 0)


def summed_on_arrival(value, axis, dim):
    blocks = in_blocks(value, dim, lax.axis_size(axis))
    arrived = lax.all_to_all(blocks, axis, split_axis=0, concat_axis=0, tiled=True)
    return arrived.astype(jnp.float32).sum(axis=0)


def split_length(length):
    first = 2 ** ((length.bit_length() - 1) // 2)
    return (first, length // first)


def small_table(size):
    index = jnp.arange(size, dtype=jnp.int32)
    product = index[:, None] * index[None, :] % size
    angles = product.astype(jnp.float32) * (2.0 * math.pi / size)
    return (jnp.cos(angles), jnp.sin(angles))


def twiddles(first, second, length):
    rows = jnp.arange(first, dtype=jnp.int32)
    cols = jnp.arange(second, dtype=jnp.int32)
    product = rows[:, None] * cols[None, :] % length
    angles = product.astype(jnp.float32) * (2.0 * math.pi / length)
    return (jnp.cos(angles), jnp.sin(angles))


def contract_last(values, table):
    return jnp.einsum(
        "mbkv,vq->mbkq",
        values,
        table,
        precision=lax.Precision.HIGHEST,
        preferred_element_type=jnp.float32,
    )


def contract_third(values, table):
    return jnp.einsum(
        "mbuv,uk->mbkv",
        values,
        table,
        precision=lax.Precision.HIGHEST,
        preferred_element_type=jnp.float32,
    )


def dispersed(values, phase_rows, length):
    first, second = split_length(length)
    cos_first, sin_first = small_table(first)
    cos_second, sin_second = small_table(second)
    twist_cos, twist_sin = twiddles(first, second, length)
    modes_here = values.shape[0]
    batch = values.shape[1]
    real_part = values[:, :, 0].reshape(modes_here, batch, first, second)
    imag_part = values[:, :, 1].reshape(modes_here, batch, first, second)
    section_re = contract_third(real_part, cos_first) + contract_third(imag_part, sin_first)
    section_im = contract_third(imag_part, cos_first) - contract_third(real_part, sin_first)
    turned_re = section_re * twist_cos + section_im * twist_sin
    turned_im = section_im * twist_cos - section_re * twist_sin
    freq_re = contract_last(turned_re, cos_second) + contract_last(turned_im, sin_second)
    freq_im = contract_last(turned_im, cos_second) - contract_last(turned_re, sin_second)
    ordered = jnp.transpose(phase_rows.reshape(modes_here, second, first), (0, 2, 1))[:, None]
    phase_cos = jnp.cos(ordered)
    phase_sin = jnp.sin(ordered)
    spun_re = freq_re * phase_cos - freq_im * phase_sin
    spun_im = freq_re * phase_sin + freq_im * phase_cos
    back_re = contract_last(spun_re, cos_second) - contract_last(spun_im, sin_second)
    back_im = contract_last(spun_im, cos_second) + contract_last(spun_re, sin_second)
    again_re = back_re * twist_cos - back_im * twist_sin
    again_im = back_im * twist_cos + back_re * twist_sin
    out_re = contract_third(again_re, cos_first) - contract_third(again_im, sin_first)
    out_im = contract_third(again_im, cos_first) + contract_third(again_re, sin_first)
    out_re = out_re.reshape(modes_here, batch, length) / length
    out_im = out_im.reshape(modes_here, batch, length) / length
    return jnp.stack([out_re, out_im], axis=2)


def body(fields, profiles, phase):
    mode_local = fields.shape[0]
    batch = fields.shape[1]
    time_local = fields.shape[3]
    pixel_local = profiles.shape[0]
    length = time_local * lax.axis_size("tm")
    scale = 1.0 / math.sqrt(pixel_local * lax.axis_size("pix"))
    modal = fields.astype(jnp.bfloat16)
    piece = gathered_copies(modal, "pix", 0)
    columns = profiles
    spatial = jnp.dot(
        columns, piece.reshape(piece.shape[0], -1), preferred_element_type=jnp.float32
    )
    spatial = spatial.reshape(pixel_local, batch, 2, time_local)
    real_part = spatial[:, :, 0]
    imag_part = spatial[:, :, 1]
    power = real_part * real_part + imag_part * imag_part
    nonlin = (
        jnp.stack([power * real_part, power * imag_part], axis=2)
        .astype(jnp.bfloat16)
        .reshape(pixel_local, -1)
    )
    columns = profiles
    kerr = summed_on_arrival(
        lax.dot_general(
            columns, nonlin, (((0,), (0,)), ((), ())), preferred_element_type=jnp.float32
        ).astype(jnp.bfloat16),
        "pix",
        0,
    )
    kerr = kerr.reshape(mode_local, batch, 2, time_local) * scale
    stepped = jnp.stack([fields[:, :, 0] - kerr[:, :, 1], fields[:, :, 1] + kerr[:, :, 0]], axis=2)
    result = dispersed(
        lax.all_to_all(stepped, "tm", split_axis=0, concat_axis=3, tiled=True), phase, length
    )
    return lax.all_to_all(result, "tm", split_axis=3, concat_axis=0, tiled=True)


def solution(mesh):
    return jax.shard_map(
        body,
        mesh=mesh,
        in_specs=(P("pix", None, None, "tm"), P("pix", None), P(("pix", "tm"), None)),
        out_specs=P("pix", None, None, "tm"),
        check_vma=False,
    )
```

profile of v0, /device:TPU:1, one launch (start us, length us, event | category | flops | bytes accessed | tf_op | source)
XLA Modules:
  0.0 126.4 jit_solution(6760236970866442374)
XLA Ops:
  0.0 0.0 copy-start
  0.0 1.0 convert_element_type.76
  1.0 0.9 broadcast_in_dim.2
  1.9 35.3 %all_to_all.46 = bf16[32,8,8,2,128]{4,3,2,1,0:T(2,128)(2,1)S(1)} all-to-all(bf16[32,8,8,2,128]{4,3,2,1,0:T(2,128)(2,1)S(1)} %broadcast_in_dim.2), channel_id=1, replica_groups=mesh['pix'=32,'tm'=8] {'pix'}, dimensions={0} | all-to-all | bytes 2097152 | tf_op jit(solution)/shard_map/all_to_all | solution.py:16
  37.2 0.8 reshape_reshape.3
  38.0 0.5 copy.59
  38.5 0.0 copy-done
  38.6 2.4 %fusion.7 = f32[2048,8,2,128]{0,3,2,1:T(8,128)S(1)} fusion(bf16[8,2,128,256]{3,2,1,0:T(8,128)(2,1)S(1)} %bitcast.110, bf16[2048,256]{1,0:T(8,128)(2,1)S(1)} %copy-done), kind=kOutput, calls=%fused_computation.21 | convolution fusion | flops 2147483648 | bytes 18874368 | tf_op jit(solution)/shard_map/dot_general | solution.py:118
  40.9 3.7 %multiply_convert_fusion.1 = (bf16[2048,8,1,128]{0,3,2,1:T(8,128)(2,1)S(1)}, bf16[2048,8,1,128]{0,3,2,1:T(8,128)(2,1)}) fusion(f32[2048,8,2,128]{0,3,2,1:T(8,128)S(1)} %fusion.7), kind=kLoop, calls=%fused_computation.2 | loop fusion | flops 14680064 | bytes 25165824 | tf_op jit(solution)/shard_map/convert
  44.7 6.2 %pad_maximum_fusion = bf16[2048,8,2,128]{0,3,2,1:T(8,128)(2,1)} fusion(bf16[2048,8,1,128]{0,3,2,1:T(8,128)(2,1)} %get-tuple-element.10, bf16[2048,8,1,128]{0,3,2,1:T(8,128)(2,1)S(1)} %get-tuple-element.9), kind=kLoop, calls=%fused_computation | loop fusion | flops 4194304 | bytes 16777216 | tf_op jit(solution)/shard_map/stack | solution.py:126
  50.8 0.0 copy-start.1
  50.8 0.0 copy-start.2
  50.8 6.9 %fusion = bf16[32,8,2048]{2,1,0:T(8,128)(2,1)} fusion(bf16[2048,2048]{0,1:T(8,128)(2,1)} %bitcast.109, bf16[2048,256]{1,0:T(8,128)(2,1)S(1)} %copy-done), kind=kOutput, calls=%fused_computation.5 | convolution fusion | flops 2148007936 | bytes 10485760 | tf_op jit(solution)/shard_map/dot_general | solution.py:132
  57.7 4.5 %all-to-all-start.1 = ((bf16[32,8,2048]{2,1,0:T(8,128)(2,1)}), bf16[32,8,2048]{2,1,0:T(8,128)(2,1)S(1)}, u32[]{:S(2)}, u32[]{:S(2)}) async-start(bf16[32,8,2048]{2,1,0:T(8,128)(2,1)} %fusion), calls=%async_computation.1 | async-start | bytes 2097152 | tf_op jit(solution)/shard_map/all_to_all | solution.py:33
  62.2 0.1 fusion.49
  62.3 15.6 %all-to-all-done.1 = bf16[32,8,2048]{2,1,0:T(8,128)(2,1)S(1)} async-done(((bf16[32,8,2048]{2,1,0:T(8,128)(2,1)}), bf16[32,8,2048]{2,1,0:T(8,128)(2,1)S(1)}, u32[]{:S(2)}, u32[]{:S(2)}) %all-to-all-start.1) | async-done | bytes 1048608 | tf_op jit(solution)/shard_map/all_to_all | solution.py:33
  77.9 0.2 convert_reduce_fusion
  78.1 0.1 mul.374
  78.2 0.0 copy-done.1
  78.2 0.1 slice_subtract_fusion
  78.2 0.7 pad_maximum_fusion.1
  78.9 21.8 %all-to-all-start.2 = ((f32[8,8,2,128]{3,2,1,0:T(2,128)}), f32[8,8,2,128]{3,2,1,0:T(2,128)S(1)}, u32[]{:S(2)}, u32[]{:S(2)}) async-start(f32[8,8,2,128]{3,2,1,0:T(2,128)} %pad_maximum_fusion.1), calls=%async_computation.2 | async-start | bytes 131072 | tf_op jit(solution)/shard_map/all_to_all | solution.py:141
  100.7 0.1 fusion.48
  100.8 0.1 copy.61
  100.9 0.1 copy.62
  101.0 0.0 copy-done.2
  101.0 0.2 cosine_reduce_fusion
  101.1 0.1 cos.51
  101.2 0.1 copy.65
  101.3 0.1 sin.51
  101.3 0.1 copy.68
  101.4 4.4 %all-to-all-done.2 = f32[8,8,2,128]{3,2,1,0:T(2,128)S(1)} async-done(((f32[8,8,2,128]{3,2,1,0:T(2,128)}), f32[8,8,2,128]{3,2,1,0:T(2,128)S(1)}, u32[]{:S(2)}, u32[]{:S(2)}) %all-to-all-start.2) | async-done | bytes 65568 | tf_op jit(solution)/shard_map/all_to_all | solution.py:141
  105.8 0.2 slice_reduce_fusion
  106.0 0.1 reshape.185
  106.1 0.3 fusion.37
  106.4 0.1 reshape.184
  106.5 0.3 fusion.39
  106.9 0.3 fusion.1
  107.2 0.3 fusion.2
  107.6 0.3 fusion.10
  107.9 0.3 fusion.12
  108.3 0.3 convolution_add_fusion.2
  108.6 0.3 convolution_subtract_fusion.2
  109.0 0.3 fusion.16
  109.3 0.3 fusion.15
  109.6 0.3 convolution_add_fusion.1
  110.0 0.3 convolution_subtract_fusion.1
  110.3 0.4 fusion.17
  110.7 0.3 fusion.18
  111.0 0.3 fusion.4
  111.4 0.1 div.21
  111.5 0.4 fusion.6
  111.9 0.1 div.25
  112.0 0.5 copy.75
  112.5 1.6 %reshape.213 = f32[8,1,2048]{2,1,0:T(1,128)S(1)} reshape(f32[1024,1,2,8]{3,2,1,0:T(2,128)S(1)} %bitcast.112) | data formatting | bytes 131072
  114.1 8.3 %all_to_all.47 = f32[8,1,2048]{2,1,0:T(1,128)S(1)} all-to-all(f32[8,1,2048]{2,1,0:T(1,128)S(1)} %reshape.213), channel_id=1, replica_groups=mesh['pix'=32,'tm'=8] {'tm'}, dimensions={0} | all-to-all | bytes 131072 | tf_op jit(solution)/shard_map/all_to_all | solution.py:143
  122.4 0.5 broadcast.240
  122.9 0.8 reduce.12
  123.7 1.6 %reshape.214 = f32[1024,1,2,8]{3,2,1,0:T(2,128)S(1)} reshape(f32[8,2048]{1,0:T(8,128)S(1)} %reduce.12) | data formatting | bytes 131072
  125.3 0.4 copy.76
  125.8 0.7 copy.77
  (3 shorter events, 0.0 us)
Async XLA Ops:
  0.0 38.5 %copy-start = (bf16[2048,256]{1,0:T(8,128)(2,1)S(1)}, bf16[2048,256]{1,0:T(8,128)(2,1)}, u32[]{:S(2)}) copy-start(bf16[2048,256]{1,0:T(8,128)(2,1)} %param.4) | copy-start | bytes 3145732
  50.8 27.3 %copy-start.1 = (f32[8,8,2,128]{3,2,1,0:T(2,128)S(1)}, f32[8,8,2,128]{3,2,1,0:T(2,128)}, u32[]{:S(2)}) copy-start(f32[8,8,2,128]{3,2,1,0:T(2,128)} %param.3) | copy-start | bytes 196612
  50.8 50.1 %copy-start.2 = (f32[1,1024]{1,0:T(1,128)S(1)}, f32[1,1024]{1,0:T(1,128)}, u32[]{:S(2)}) copy-start(f32[1,1024]{1,0:T(1,128)} %param.5) | copy-start | bytes 12292
  57.7 20.2 %all-to-all-start.1 = ((bf16[32,8,2048]{2,1,0:T(8,128)(2,1)}), bf16[32,8,2048]{2,1,0:T(8,128)(2,1)S(1)}, u32[]{:S(2)}, u32[]{:S(2)}) async-start(bf16[32,8,2048]{2,1,0:T(8,128)(2,1)} %fusion), calls=%async_computation.1 | async-start | bytes 2097152 | tf_op jit(solution)/shard_map/all_to_all | solution.py:33
  78.9 26.9 %all-to-all-start.2 = ((f32[8,8,2,128]{3,2,1,0:T(2,128)}), f32[8,8,2,128]{3,2,1,0:T(2,128)S(1)}, u32[]{:S(2)}, u32[]{:S(2)}) async-start(f32[8,8,2,128]{3,2,1,0:T(2,128)} %pad_maximum_fusion.1), calls=%async_computation.2 | async-start | bytes 131072 | tf_op jit(solution)/shard_map/all_to_all | solution.py:141
where the time goes:
time: 127 us; the launch traced here: 126 us
  blocking collectives  43.6 us (34%)
  starting transfers between devices  26.3 us (21%)
  waiting for transfers between devices  20 us (16%)
  matrix products  14.7 us (12%)
  other arithmetic  12.7 us (10%)
  local copies, waits for them, and re-layouts  8.85 us (7%)
    all_to_all x1, blocking collectives, copy_for_each(): lax.all_to_all(jnp.broadcast_to(value[None], (devices, *value.shape)), ax...  35.3 us
    all_to_all x1, starting transfers between devices, body(): lax.all_to_all(stepped, 'tm', split_axis=0, concat_axis=3, tiled=True)  21.8 us
    all_to_all x1, waiting for transfers between devices, summed_on_arrival(): lax.all_to_all(blocks, axis, split_axis=0, concat_axis=0, tiled=True)  15.6 us
    all_to_all x1, blocking collectives, body(): return lax.all_to_all(result, 'tm', split_axis=3, concat_axis=0, tiled=True)  8.29 us
    dot_general x1, matrix products, body(): lax.dot_general(columns, nonlin, (((0,), (0,)), ((), ())), preferred_elem...  6.85 us
    another operation x1, other arithmetic, body(): jnp.stack([power * real_part, power * imag_part], axis=2)  6.18 us
    all_to_all x1, starting transfers between devices, summed_on_arrival(): lax.all_to_all(blocks, axis, split_axis=0, concat_axis=0, tiled=True)  4.52 us
    all_to_all x1, waiting for transfers between devices, body(): lax.all_to_all(stepped, 'tm', split_axis=0, concat_axis=3, tiled=True)  4.38 us
  transfers between devices with their start and end apart: 2, of which 2 were waited for; matrix products, arithmetic and copies ran while one was open for 1% of the time, Pallas kernels for 0%

commit v1 on v0

--- a/solution.py
+++ b/solution.py
@@ -138,7 +138,17 @@
     kerr = kerr.reshape(mode_local, batch, 2, time_local) * scale
     stepped = jnp.stack([fields[:, :, 0] - kerr[:, :, 1], fields[:, :, 1] + kerr[:, :, 0]], axis=2)
     result = dispersed(
-        lax.all_to_all(stepped, "tm", split_axis=0, concat_axis=3, tiled=True), phase, length
+        jnp.concatenate(
+            lax.all_to_all(
+                jnp.stack(jnp.split(stepped, lax.axis_size("tm"), axis=0), axis=0),
+                "tm",
+                split_axis=0,
+                concat_axis=0,
+            ),
+            axis=3,
+        ),
+        phase,
+        length,
     )
     return lax.all_to_all(result, "tm", split_axis=3, concat_axis=0, tiled=True)
 

time: 127 us -> 131 us (1.031)
  local copies, waits for them, and re-layouts: 8.85 us -> 13.6 us
    unnamed x8 -> x15, local copies, waits for them, and re-layouts: 3.19 us -> 7.39 us
where the time goes in v1:
time: 131 us
  blocking collectives  43.6 us (33%)
  starting transfers between devices  26.3 us (20%)
  waiting for transfers between devices  20 us (15%)
  matrix products  14.7 us (11%)
  local copies, waits for them, and re-layouts  13.6 us (10%)
  other arithmetic  12.1 us (9%)
    all_to_all x1, blocking collectives, copy_for_each(): lax.all_to_all(jnp.broadcast_to(value[None], (devices, *value.shape)), ax...  35.3 us
    all_to_all x1, starting transfers between devices, body(): lax.all_to_all(jnp.stack(jnp.split(stepped, lax.axis_size('tm'), axis=0),...  21.8 us
    all_to_all x1, waiting for transfers between devices, summed_on_arrival(): lax.all_to_all(blocks, axis, split_axis=0, concat_axis=0, tiled=True)  15.6 us
    all_to_all x1, blocking collectives, body(): return lax.all_to_all(result, 'tm', split_axis=3, concat_axis=0, tiled=True)  8.29 us
    unnamed x15, local copies, waits for them, and re-layouts  7.39 us
    dot_general x1, matrix products, body(): lax.dot_general(columns, nonlin, (((0,), (0,)), ((), ())), preferred_elem...  6.85 us
    another operation x1, other arithmetic, body(): jnp.stack([power * real_part, power * imag_part], axis=2)  6.18 us
    all_to_all x1, starting transfers between devices, summed_on_arrival(): lax.all_to_all(blocks, axis, split_axis=0, concat_axis=0, tiled=True)  4.52 us
  transfers between devices with their start and end apart: 2, of which 2 were waited for; matrix products, arithmetic and copies ran while one was open for 1% of the time, Pallas kernels for 0%

profile of v1, /device:TPU:1, one launch (start us, length us, event | category | flops | bytes accessed | tf_op | source)
XLA Modules:
  0.0 130.6 jit_solution(15973376103596795433)
XLA Ops:
  0.0 0.0 copy-start
  0.0 1.0 convert_element_type.76
  1.0 0.9 broadcast_in_dim.2
  1.9 35.3 %all_to_all.33 = bf16[32,8,8,2,128]{4,3,2,1,0:T(2,128)(2,1)S(1)} all-to-all(bf16[32,8,8,2,128]{4,3,2,1,0:T(2,128)(2,1)S(1)} %broadcast_in_dim.2), channel_id=1, replica_groups=mesh['pix'=32,'tm'=8] {'pix'}, dimensions={0} | all-to-all | bytes 2097152 | tf_op jit(solution)/shard_map/all_to_all | solution.py:16
  37.2 0.8 reshape_reshape.3
  38.0 0.5 copy.71
  38.6 2.4 %fusion.7 = f32[2048,8,2,128]{0,3,2,1:T(8,128)S(1)} fusion(bf16[8,2,128,256]{3,2,1,0:T(8,128)(2,1)S(1)} %bitcast.130, bf16[2048,256]{1,0:T(8,128)(2,1)S(1)} %copy-done), kind=kOutput, calls=%fused_computation.21 | convolution fusion | flops 2147483648 | bytes 18874368 | tf_op jit(solution)/shard_map/dot_general | solution.py:118
  40.9 3.7 %multiply_convert_fusion.1 = (bf16[2048,8,1,128]{0,3,2,1:T(8,128)(2,1)S(1)}, bf16[2048,8,1,128]{0,3,2,1:T(8,128)(2,1)}) fusion(f32[2048,8,2,128]{0,3,2,1:T(8,128)S(1)} %fusion.7), kind=kLoop, calls=%fused_computation.2 | loop fusion | flops 14680064 | bytes 25165824 | tf_op jit(solution)/shard_map/convert
  44.7 6.2 %pad_maximum_fusion = bf16[2048,8,2,128]{0,3,2,1:T(8,128)(2,1)} fusion(bf16[2048,8,1,128]{0,3,2,1:T(8,128)(2,1)} %get-tuple-element.10, bf16[2048,8,1,128]{0,3,2,1:T(8,128)(2,1)S(1)} %get-tuple-element.9), kind=kLoop, calls=%fused_computation | loop fusion | flops 4194304 | bytes 16777216 | tf_op jit(solution)/shard_map/stack | solution.py:126
  50.8 6.9 %fusion = bf16[32,8,2048]{2,1,0:T(8,128)(2,1)} fusion(bf16[2048,2048]{0,1:T(8,128)(2,1)} %bitcast.129, bf16[2048,256]{1,0:T(8,128)(2,1)S(1)} %copy-done), kind=kOutput, calls=%fused_computation.5 | convolution fusion | flops 2148007936 | bytes 10485760 | tf_op jit(solution)/shard_map/dot_general | solution.py:132
  57.7 4.5 %all-to-all-start.1 = ((bf16[32,8,2048]{2,1,0:T(8,128)(2,1)}), bf16[32,8,2048]{2,1,0:T(8,128)(2,1)S(1)}, u32[]{:S(2)}, u32[]{:S(2)}) async-start(bf16[32,8,2048]{2,1,0:T(8,128)(2,1)} %fusion), calls=%async_computation.1 | async-start | bytes 2097152 | tf_op jit(solution)/shard_map/all_to_all | solution.py:33
  62.2 0.1 fusion.56
  62.3 15.6 %all-to-all-done.1 = bf16[32,8,2048]{2,1,0:T(8,128)(2,1)S(1)} async-done(((bf16[32,8,2048]{2,1,0:T(8,128)(2,1)}), bf16[32,8,2048]{2,1,0:T(8,128)(2,1)S(1)}, u32[]{:S(2)}, u32[]{:S(2)}) %all-to-all-start.1) | async-done | bytes 1048608 | tf_op jit(solution)/shard_map/all_to_all | solution.py:33
  77.9 0.2 convert_reduce_fusion
  78.1 0.1 mul.374
  78.2 0.1 slice_add_fusion
  78.2 0.1 pad_maximum_fusion.2
  78.3 0.6 constant_dynamic-update-slice_fusion.7
  78.9 0.6 constant_dynamic-update-slice_fusion.6
  79.5 0.6 constant_dynamic-update-slice_fusion.5
  80.1 0.6 constant_dynamic-update-slice_fusion.4
  80.7 0.6 constant_dynamic-update-slice_fusion.3
  81.3 0.6 constant_dynamic-update-slice_fusion.2
  81.9 0.6 constant_dynamic-update-slice_fusion.1
  82.5 0.6 constant_dynamic-update-slice_fusion
  83.1 21.8 %all-to-all-start.2 = ((f32[8,1,8,2,128]{4,1,3,2,0:T(1,128)}), f32[8,1,8,2,128]{4,1,3,2,0:T(1,128)S(1)}, u32[]{:S(2)}, u32[]{:S(2)}) async-start(f32[8,1,8,2,128]{4,1,3,2,0:T(1,128)} %constant_dynamic-update-slice_fusion), calls=%async_computation.2 | async-start | bytes 131072 | tf_op jit(solution)/shard_map/all_to_all | solution.py:142
  104.9 0.1 fusion.55
  105.0 0.1 copy.80
  105.1 0.1 copy.81
  105.1 0.2 cosine_reduce_fusion
  105.3 0.1 cos.51
  105.4 0.1 copy.84
  105.4 0.1 sin.51
  105.5 0.1 copy.87
  105.6 4.4 %all-to-all-done.2 = f32[8,1,8,2,128]{4,1,3,2,0:T(1,128)S(1)} async-done(((f32[8,1,8,2,128]{4,1,3,2,0:T(1,128)}), f32[8,1,8,2,128]{4,1,3,2,0:T(1,128)S(1)}, u32[]{:S(2)}, u32[]{:S(2)}) %all-to-all-start.2) | async-done | bytes 65568 | tf_op jit(solution)/shard_map/all_to_all | solution.py:142
  110.0 0.2 slice_reduce_fusion
  110.2 0.1 reshape.193
  110.3 0.3 fusion.37
  110.6 0.1 reshape.192
  110.7 0.3 fusion.39
  111.1 0.3 fusion.1
  111.4 0.3 fusion.2
  111.8 0.3 fusion.10
  112.1 0.3 fusion.12
  112.4 0.3 convolution_add_fusion.2
  112.8 0.3 convolution_subtract_fusion.2
  113.1 0.3 fusion.16
  113.5 0.3 fusion.15
  113.8 0.3 convolution_add_fusion.1
  114.2 0.3 convolution_subtract_fusion.1
  114.5 0.4 fusion.17
  114.9 0.3 fusion.18
  115.2 0.3 fusion.4
  115.6 0.1 div.21
  115.7 0.4 fusion.6
  116.0 0.1 div.25
  116.2 0.5 copy.94
  116.7 1.6 %reshape.221 = f32[8,1,2048]{2,1,0:T(1,128)S(1)} reshape(f32[1024,1,2,8]{3,2,1,0:T(2,128)S(1)} %bitcast.132) | data formatting | bytes 131072
  118.3 8.3 %all_to_all.34 = f32[8,1,2048]{2,1,0:T(1,128)S(1)} all-to-all(f32[8,1,2048]{2,1,0:T(1,128)S(1)} %reshape.221), channel_id=1, replica_groups=mesh['pix'=32,'tm'=8] {'tm'}, dimensions={0} | all-to-all | bytes 131072 | tf_op jit(solution)/shard_map/all_to_all | solution.py:153
  126.6 0.5 broadcast.240
  127.1 0.8 reduce.12
  127.9 1.6 %reshape.222 = f32[1024,1,2,8]{3,2,1,0:T(2,128)S(1)} reshape(f32[8,2048]{1,0:T(8,128)S(1)} %reduce.12) | data formatting | bytes 131072
  129.5 0.4 copy.95
  129.9 0.7 copy.96
  (8 shorter events, 0.0 us)
Async XLA Ops:
  0.0 38.5 %copy-start = (bf16[2048,256]{1,0:T(8,128)(2,1)S(1)}, bf16[2048,256]{1,0:T(8,128)(2,1)}, u32[]{:S(2)}) copy-start(bf16[2048,256]{1,0:T(8,128)(2,1)} %param.4) | copy-start | bytes 3145732
  50.8 27.3 %copy-start.1 = (f32[8,8,2,128]{3,2,1,0:T(2,128)S(1)}, f32[8,8,2,128]{3,2,1,0:T(2,128)}, u32[]{:S(2)}) copy-start(f32[8,8,2,128]{3,2,1,0:T(2,128)} %param.3) | copy-start | bytes 196612
  50.8 54.3 %copy-start.2 = (f32[1,1024]{1,0:T(1,128)S(1)}, f32[1,1024]{1,0:T(1,128)}, u32[]{:S(2)}) copy-start(f32[1,1024]{1,0:T(1,128)} %param.5) | copy-start | bytes 12292
  57.7 20.2 %all-to-all-start.1 = ((bf16[32,8,2048]{2,1,0:T(8,128)(2,1)}), bf16[32,8,2048]{2,1,0:T(8,128)(2,1)S(1)}, u32[]{:S(2)}, u32[]{:S(2)}) async-start(bf16[32,8,2048]{2,1,0:T(8,128)(2,1)} %fusion), calls=%async_computation.1 | async-start | bytes 2097152 | tf_op jit(solution)/shard_map/all_to_all | solution.py:33
  83.1 26.9 %all-to-all-start.2 = ((f32[8,1,8,2,128]{4,1,3,2,0:T(1,128)}), f32[8,1,8,2,128]{4,1,3,2,0:T(1,128)S(1)}, u32[]{:S(2)}, u32[]{:S(2)}) async-start(f32[8,1,8,2,128]{4,1,3,2,0:T(1,128)} %constant_dynamic-update-slice_fusion), calls=%async_computation.2 | async-start | bytes 131072 | tf_op jit(solution)/shard_map/all_to_all | solution.py:142
